TPU v7x, 512 devices: a whole 4x4x16 slice. The times are simulated.
512 devices in a mesh: grp: 16 (over x_lo, y, core), dev: 32 (over x_hi, z).
Axes of the slice: x: 4 (x_hi: 2, x_lo: 2; x = x_hi * 2 + x_lo), y: 4, z: 16, core: 2. Of those that a mesh axis runs over, the one named last changes fastest.
Arguments:
- voltage: float32 [2, 4096, 4192], P(None, ('grp', 'dev')), may hold values from -6 to 6
- filter_taps: float32 [4, 32], replicated, may hold values from -0.5 to 0.5
- plan: int32 [16, 9], P('grp'), may hold values from 0 to 8, each once within a row
Outputs:
- visibility: bfloat16 [16, 9, 32, 2, 256, 256], P('grp', None, 'dev')
Inputs may be any that keep to these rules, and one draw needn't show every extreme that they name: Each row of plan holds every distance 0 to 8 once.
All inputs are finite; a program needn't handle non-finite values.
Results may differ from a plain program's by a relative error of at most 0.0056.
Values may be sent and summed in bfloat16 or wider, within the bound.
No kernel may reach another device: no remote copies, remote signals or barrier semaphores. Data moves between devices by JAX's collectives and lax.ppermute only.
A program may use at most 64 MiB of HBM per device.

v0:
```python
import math

import jax
import jax.numpy as jnp
from jax import lax
from jax.sharding import PartitionSpec as P

F = 32
TAPS = 4
SPECTRA = 128
FRAMES = 131


def shifted(x, axis, by):
    length = lax.axis_size(axis)
    return lax.ppermute(x, axis, [(i, (i + by) % length) for i in range(length)])


def compute_spectra(voltage, filter_taps):
    signal_input_count = voltage.shape[1]
    framed_samples = voltage.reshape(2, signal_input_count, FRAMES, F)
    filtered = filter_taps[0][None, None, None, :] * framed_samples[:, :, 0:SPECTRA, :]
    for p in range(1, TAPS):
        filtered = (
            filtered
            + filter_taps[p][None, None, None, :] * framed_samples[:, :, p : p + SPECTRA, :]
        )
    indices = jnp.arange(F, dtype=jnp.int32)
    phase_angle = (indices[:, None] * indices[None, :] % F).astype(jnp.float32) * (
        2.0 * math.pi / F
    )
    cosine_table = jnp.cos(phase_angle)
    sine_table = jnp.sin(phase_angle)
    highest = lax.Precision.HIGHEST
    real_part = jnp.einsum(
        "csn,nf->fcs", filtered[0], cosine_table, precision=highest
    ) + jnp.einsum("csn,nf->fcs", filtered[1], sine_table, precision=highest)
    imaginary_component = jnp.einsum(
        "csn,nf->fcs", filtered[1], cosine_table, precision=highest
    ) - jnp.einsum("csn,nf->fcs", filtered[0], sine_table, precision=highest)
    return jnp.stack([real_part, imaginary_component], axis=2).astype(jnp.bfloat16)


def correlate(own_block, partner):
    chans, rows_here = (own_block.shape[0], own_block.shape[1])
    left_spectrum_rows = own_block.reshape(chans, rows_here, -1)
    real_part = partner[:, :, 0, :]
    imaginary_component = partner[:, :, 1, :]
    right_spectrum_rows = jnp.stack(
        [
            jnp.concatenate([real_part, imaginary_component], -1),
            jnp.concatenate([-imaginary_component, real_part], -1),
        ],
        axis=1,
    )
    cross_products = jnp.einsum(
        "gzi,gkvi->gkzv",
        left_spectrum_rows,
        right_spectrum_rows,
        preferred_element_type=jnp.float32,
    )
    return (cross_products / SPECTRA).astype(jnp.bfloat16)


def per_device(voltage, filter_taps, plan):
    local_spectra = compute_spectra(voltage, filter_taps)
    own_block = lax.all_to_all(local_spectra, "dev", split_axis=0, concat_axis=1, tiled=True)
    groups = lax.axis_size("grp")
    rounds = groups // 2 + 1
    results = [correlate(own_block, own_block)]
    received = own_block
    for distance in range(1, rounds):
        received = shifted(own_block, "grp", distance)
        results.append(correlate(own_block, received))
    stacked = jnp.stack(results, axis=0)
    return jnp.take(stacked, plan[0], axis=0)[None]


def solution(mesh):
    return jax.shard_map(
        per_device,
        mesh=mesh,
        in_specs=(P(None, ("grp", "dev"), None), P(), P("grp", None)),
        out_specs=P("grp", None, "dev", None, None, None),
        check_vma=False,
    )
```

profile of v0, /device:TPU:1, one launch (start us, length us, event | category | flops | bytes accessed | tf_op | source)
XLA Modules:
  0.0 89.8 jit_solution(14616734474427329352)
XLA Ops:
  0.0 1.3 %reshape.257 = f32[2,8,131,32]{3,2,1,0:T(8,128)S(1)} reshape(f32[2,8,4192]{2,1,0:T(8,128)} %param.3) | data formatting | bytes 536576 | tf_op jit(solution)/shard_map/reshape | solution.py:21
  1.3 1.8 %fusion.111 = (f32[2,8,128,32]{3,2,1,0:T(8,128)S(1)}, f32[2,8,128,32]{3,2,1,0:T(8,128)}, f32[2,8,128,32]{3,2,1,0:T(8,128)S(1)}, f32[2,8,128,32]{3,2,1,0:T(8,128)}) fusion(f32[2,8,131,32]{3,2,1,0:T(8,128)S(1)} %reshape.257), kind=kLoop, calls=%fused_computation.181 | loop fusion | bytes 2097152 | tf_op jit(solution)/shard_map/slice | solution.py:22
  3.1 0.0 copy-start.1
  3.1 1.5 %copy.22 = f32[2,8,128,32]{2,3,1,0:T(8,128)S(1)} copy(f32[2,8,128,32]{3,2,1,0:T(8,128)} %get-tuple-element.8) | data formatting | bytes 524288
  4.6 1.5 %copy.21 = f32[2,8,128,32]{2,3,1,0:T(8,128)S(1)} copy(f32[2,8,128,32]{3,2,1,0:T(8,128)} %get-tuple-element.6) | data formatting | bytes 524288
  6.2 0.3 copy.20
  6.5 0.0 copy-start.2
  6.5 0.3 copy.19
  6.8 0.0 copy-done.1
  6.8 0.2 multiply_add_fusion
  7.0 0.3 fusion.59
  7.3 0.3 fusion.58
  7.7 0.3 fusion.29
  8.0 0.3 fusion.30
  8.4 0.7 copy.16
  9.1 18.5 %all-to-all-start = ((bf16[32,8,2,128]{3,1,2,0:T(8,128)(2,1)}), bf16[32,8,2,128]{3,1,2,0:T(8,128)(2,1)S(1)}, u32[]{:S(2)}, u32[]{:S(2)}) async-start(bf16[32,8,2,128]{3,1,2,0:T(8,128)(2,1)} %copy.16), calls=%async_computation | async-start | bytes 262144 | tf_op jit(solution)/shard_map/all_to_all | solution.py:67
  27.6 0.0 copy-done.2
  27.6 16.3 %all-to-all-done = bf16[32,8,2,128]{3,1,2,0:T(8,128)(2,1)S(1)} async-done(((bf16[32,8,2,128]{3,1,2,0:T(8,128)(2,1)}), bf16[32,8,2,128]{3,1,2,0:T(8,128)(2,1)S(1)}, u32[]{:S(2)}, u32[]{:S(2)}) %all-to-all-start) | async-done | bytes 131104 | tf_op jit(solution)/shard_map/all_to_all | solution.py:67
  44.0 6.1 %collective-permute-start = (bf16[1,256,2,128]{3,1,2,0:T(8,128)(2,1)S(1)}, bf16[1,256,2,128]{3,1,2,0:T(8,128)(2,1)S(1)}, u32[]{:S(2)}, u32[]{:S(2)}) collective-permute-start(bf16[1,256,2,128]{3,1,2,0:T(8,128)(2,1)S(1)} %bitcast.255), channel_id=1, source_target_pairs={{0,32},{32,64},{64,96},{96,128},{128,160},{160,192},{192,224},{224... | collective-permute-start | bytes 393224 | tf_op jit(solution)/shard_map/ppermute | solution.py:16
  50.1 3.2 %collective-permute-start.1 = (bf16[1,256,2,128]{3,1,2,0:T(8,128)(2,1)S(1)}, bf16[1,256,2,128]{3,1,2,0:T(8,128)(2,1)S(1)}, u32[]{:S(2)}, u32[]{:S(2)}) collective-permute-start(bf16[1,256,2,128]{3,1,2,0:T(8,128)(2,1)S(1)} %bitcast.256), channel_id=1, source_target_pairs={{0,64},{32,96},{64,128},{96,160},{128,192},{160,224},{192,256},{22... | collective-permute-start | bytes 393224 | tf_op jit(solution)/shard_map/ppermute | solution.py:16
  53.3 3.5 %collective-permute-start.2 = (bf16[1,256,2,128]{3,1,2,0:T(8,128)(2,1)S(1)}, bf16[1,256,2,128]{3,1,2,0:T(8,128)(2,1)S(1)}, u32[]{:S(2)}, u32[]{:S(2)}) collective-permute-start(bf16[1,256,2,128]{3,1,2,0:T(8,128)(2,1)S(1)} %bitcast.257), channel_id=1, source_target_pairs={{0,96},{32,128},{64,160},{96,192},{128,224},{160,256},{192,288},{2... | collective-permute-start | bytes 393224 | tf_op jit(solution)/shard_map/ppermute | solution.py:16
  56.8 2.3 %collective-permute-start.3 = (bf16[1,256,2,128]{3,1,2,0:T(8,128)(2,1)S(1)}, bf16[1,256,2,128]{3,1,2,0:T(8,128)(2,1)S(1)}, u32[]{:S(2)}, u32[]{:S(2)}) collective-permute-start(bf16[1,256,2,128]{3,1,2,0:T(8,128)(2,1)S(1)} %bitcast.258), channel_id=1, source_target_pairs={{0,128},{32,160},{64,192},{96,224},{128,256},{160,288},{192,320},{... | collective-permute-start | bytes 393224 | tf_op jit(solution)/shard_map/ppermute | solution.py:16
  59.1 4.7 %collective-permute-start.4 = (bf16[1,256,2,128]{3,1,2,0:T(8,128)(2,1)S(1)}, bf16[1,256,2,128]{3,1,2,0:T(8,128)(2,1)S(1)}, u32[]{:S(2)}, u32[]{:S(2)}) collective-permute-start(bf16[1,256,2,128]{3,1,2,0:T(8,128)(2,1)S(1)} %bitcast.259), channel_id=1, source_target_pairs={{0,160},{32,192},{64,224},{96,256},{128,288},{160,320},{192,352},{... | collective-permute-start | bytes 393224 | tf_op jit(solution)/shard_map/ppermute | solution.py:16
  63.8 0.3 fusion.26
  64.1 0.0 collective-permute-done
  64.1 2.8 %collective-permute-start.5 = (bf16[1,256,2,128]{3,1,2,0:T(8,128)(2,1)S(1)}, bf16[1,256,2,128]{3,1,2,0:T(8,128)(2,1)S(1)}, u32[]{:S(2)}, u32[]{:S(2)}) collective-permute-start(bf16[1,256,2,128]{3,1,2,0:T(8,128)(2,1)S(1)} %bitcast.260), channel_id=1, source_target_pairs={{0,192},{32,224},{64,256},{96,288},{128,320},{160,352},{192,384},{... | collective-permute-start | bytes 393224 | tf_op jit(solution)/shard_map/ppermute | solution.py:16
  67.0 0.0 collective-permute-done.1
  67.0 3.6 %collective-permute-start.6 = (bf16[1,256,2,128]{3,1,2,0:T(8,128)(2,1)S(1)}, bf16[1,256,2,128]{3,1,2,0:T(8,128)(2,1)S(1)}, u32[]{:S(2)}, u32[]{:S(2)}) collective-permute-start(bf16[1,256,2,128]{3,1,2,0:T(8,128)(2,1)S(1)} %bitcast.261), channel_id=1, source_target_pairs={{0,224},{32,256},{64,288},{96,320},{128,352},{160,384},{192,416},{... | collective-permute-start | bytes 393224 | tf_op jit(solution)/shard_map/ppermute | solution.py:16
  70.7 0.0 collective-permute-done.2
  70.7 3.1 %collective-permute-start.7 = (bf16[1,256,2,128]{3,1,2,0:T(8,128)(2,1)S(1)}, bf16[1,256,2,128]{3,1,2,0:T(8,128)(2,1)S(1)}, u32[]{:S(2)}, u32[]{:S(2)}) collective-permute-start(bf16[1,256,2,128]{3,1,2,0:T(8,128)(2,1)S(1)} %bitcast.262), channel_id=1, source_target_pairs={{0,256},{32,288},{64,320},{96,352},{128,384},{160,416},{192,448},{... | collective-permute-start | bytes 393224 | tf_op jit(solution)/shard_map/ppermute | solution.py:16
  73.8 0.0 collective-permute-done.3
  73.9 0.0 collective-permute-done.4
  74.0 0.0 collective-permute-done.5
  74.1 1.4 %collective-permute-done.6 = bf16[1,256,2,128]{3,1,2,0:T(8,128)(2,1)S(1)} collective-permute-done((bf16[1,256,2,128]{3,1,2,0:T(8,128)(2,1)S(1)}, bf16[1,256,2,128]{3,1,2,0:T(8,128)(2,1)S(1)}, u32[]{:S(2)}, u32[]{:S(2)}) %collective-permute-start.6) | collective-permute-done | bytes 131104 | tf_op jit(solution)/shard_map/ppermute | solution.py:16
  75.7 2.2 %collective-permute-done.7 = bf16[1,256,2,128]{3,1,2,0:T(8,128)(2,1)S(1)} collective-permute-done((bf16[1,256,2,128]{3,1,2,0:T(8,128)(2,1)S(1)}, bf16[1,256,2,128]{3,1,2,0:T(8,128)(2,1)S(1)}, u32[]{:S(2)}, u32[]{:S(2)}) %collective-permute-start.7) | collective-permute-done | bytes 131104 | tf_op jit(solution)/shard_map/ppermute | solution.py:16
  77.9 0.3 fusion.24
  78.2 0.3 fusion.22
  78.4 0.3 fusion.20
  78.7 0.3 fusion.18
  79.0 0.3 fusion.16
  79.2 0.3 fusion.14
  79.5 0.3 fusion.12
  79.8 0.3 fusion.10
  80.0 0.0 copy-start
  80.1 1.4 %copy-done = bf16[9,1,2,256,256]{3,4,2,1,0:T(8,128)(2,1)} copy-done((bf16[9,1,2,256,256]{3,4,2,1,0:T(8,128)(2,1)}, bf16[9,1,2,256,256]{3,4,2,1,0:T(8,128)(2,1)S(1)}, u32[]{:S(2)}) %copy-start) | copy-done | bytes 2359320
  81.5 2.4 %gather_fusion = bf16[9,2,256,256]{2,3,1,0:T(8,128)(2,1)S(1)} fusion(bf16[9,2,256,256]{2,3,1,0:T(8,128)(2,1)} %bitcast.252, s32[1024]{0:T(1024)S(1)} %pad_clamp_fusion), kind=kCustom, calls=%fused_computation | custom fusion | bytes 4718628 | tf_op jit(solution)/shard_map/jit(_take)/gather | solution.py:76
  83.8 1.7 %bitcast_select_fusion = bf16[1,9,1,2,256,256]{4,5,3,1,2,0:T(8,128)(2,1)} fusion(bf16[9,2,256,256]{2,3,1,0:T(8,128)(2,1)S(1)} %gather_fusion, pred[9]{0:T(512)(128)(4,1)S(1)} %compare_and_fusion), kind=kLoop, calls=%fused_computation.1 | loop fusion | flops 1179648 | bytes 4718601 | tf_op jit(solution)/shard_map/jit(_take)/select_n | solution.py:76
  85.5 4.3 %copy.18 = bf16[1,9,1,2,256,256]{5,4,3,2,1,0:T(8,128)(2,1)} copy(bf16[1,9,1,2,256,256]{4,5,3,1,2,0:T(8,128)(2,1)} %bitcast_select_fusion) | data formatting | bytes 4718592 | tf_op jit(solution)/shard_map/jit(_take)/select_n | solution.py:76
  (33 shorter events, 0.5 us)
Async XLA Ops:
  3.1 3.7 %copy-start.1 = (f32[4,32]{1,0:T(4,128)S(1)}, f32[4,32]{1,0:T(4,128)}, u32[]{:S(2)}) copy-start(f32[4,32]{1,0:T(4,128)} %param.4) | copy-start | bytes 1540
  6.5 21.1 %copy-start.2 = (s32[1,9]{1,0:T(1,128)S(1)}, s32[1,9]{1,0:T(1,128)}, u32[]{:S(2)}) copy-start(s32[1,9]{1,0:T(1,128)} %param.5) | copy-start | bytes 112
  9.1 34.8 %all-to-all-start = ((bf16[32,8,2,128]{3,1,2,0:T(8,128)(2,1)}), bf16[32,8,2,128]{3,1,2,0:T(8,128)(2,1)S(1)}, u32[]{:S(2)}, u32[]{:S(2)}) async-start(bf16[32,8,2,128]{3,1,2,0:T(8,128)(2,1)} %copy.16), calls=%async_computation | async-start | bytes 262144 | tf_op jit(solution)/shard_map/all_to_all | solution.py:67
  44.0 20.2 %collective-permute-start = (bf16[1,256,2,128]{3,1,2,0:T(8,128)(2,1)S(1)}, bf16[1,256,2,128]{3,1,2,0:T(8,128)(2,1)S(1)}, u32[]{:S(2)}, u32[]{:S(2)}) collective-permute-start(bf16[1,256,2,128]{3,1,2,0:T(8,128)(2,1)S(1)} %bitcast.255), channel_id=1, source_target_pairs={{0,32},{32,64},{64,96},{96,128},{128,160},{160,192},{192,224},{224... | collective-permute-start | bytes 393224 | tf_op jit(solution)/shard_map/ppermute | solution.py:16
  50.1 17.0 %collective-permute-start.1 = (bf16[1,256,2,128]{3,1,2,0:T(8,128)(2,1)S(1)}, bf16[1,256,2,128]{3,1,2,0:T(8,128)(2,1)S(1)}, u32[]{:S(2)}, u32[]{:S(2)}) collective-permute-start(bf16[1,256,2,128]{3,1,2,0:T(8,128)(2,1)S(1)} %bitcast.256), channel_id=1, source_target_pairs={{0,64},{32,96},{64,128},{96,160},{128,192},{160,224},{192,256},{22... | collective-permute-start | bytes 393224 | tf_op jit(solution)/shard_map/ppermute | solution.py:16
  53.3 17.4 %collective-permute-start.2 = (bf16[1,256,2,128]{3,1,2,0:T(8,128)(2,1)S(1)}, bf16[1,256,2,128]{3,1,2,0:T(8,128)(2,1)S(1)}, u32[]{:S(2)}, u32[]{:S(2)}) collective-permute-start(bf16[1,256,2,128]{3,1,2,0:T(8,128)(2,1)S(1)} %bitcast.257), channel_id=1, source_target_pairs={{0,96},{32,128},{64,160},{96,192},{128,224},{160,256},{192,288},{2... | collective-permute-start | bytes 393224 | tf_op jit(solution)/shard_map/ppermute | solution.py:16
  56.8 17.0 %collective-permute-start.3 = (bf16[1,256,2,128]{3,1,2,0:T(8,128)(2,1)S(1)}, bf16[1,256,2,128]{3,1,2,0:T(8,128)(2,1)S(1)}, u32[]{:S(2)}, u32[]{:S(2)}) collective-permute-start(bf16[1,256,2,128]{3,1,2,0:T(8,128)(2,1)S(1)} %bitcast.258), channel_id=1, source_target_pairs={{0,128},{32,160},{64,192},{96,224},{128,256},{160,288},{192,320},{... | collective-permute-start | bytes 393224 | tf_op jit(solution)/shard_map/ppermute | solution.py:16
  59.1 14.8 %collective-permute-start.4 = (bf16[1,256,2,128]{3,1,2,0:T(8,128)(2,1)S(1)}, bf16[1,256,2,128]{3,1,2,0:T(8,128)(2,1)S(1)}, u32[]{:S(2)}, u32[]{:S(2)}) collective-permute-start(bf16[1,256,2,128]{3,1,2,0:T(8,128)(2,1)S(1)} %bitcast.259), channel_id=1, source_target_pairs={{0,160},{32,192},{64,224},{96,256},{128,288},{160,320},{192,352},{... | collective-permute-start | bytes 393224 | tf_op jit(solution)/shard_map/ppermute | solution.py:16
  64.1 9.9 %collective-permute-start.5 = (bf16[1,256,2,128]{3,1,2,0:T(8,128)(2,1)S(1)}, bf16[1,256,2,128]{3,1,2,0:T(8,128)(2,1)S(1)}, u32[]{:S(2)}, u32[]{:S(2)}) collective-permute-start(bf16[1,256,2,128]{3,1,2,0:T(8,128)(2,1)S(1)} %bitcast.260), channel_id=1, source_target_pairs={{0,192},{32,224},{64,256},{96,288},{128,320},{160,352},{192,384},{... | collective-permute-start | bytes 393224 | tf_op jit(solution)/shard_map/ppermute | solution.py:16
  67.0 8.5 %collective-permute-start.6 = (bf16[1,256,2,128]{3,1,2,0:T(8,128)(2,1)S(1)}, bf16[1,256,2,128]{3,1,2,0:T(8,128)(2,1)S(1)}, u32[]{:S(2)}, u32[]{:S(2)}) collective-permute-start(bf16[1,256,2,128]{3,1,2,0:T(8,128)(2,1)S(1)} %bitcast.261), channel_id=1, source_target_pairs={{0,224},{32,256},{64,288},{96,320},{128,352},{160,384},{192,416},{... | collective-permute-start | bytes 393224 | tf_op jit(solution)/shard_map/ppermute | solution.py:16
  70.7 7.1 %collective-permute-start.7 = (bf16[1,256,2,128]{3,1,2,0:T(8,128)(2,1)S(1)}, bf16[1,256,2,128]{3,1,2,0:T(8,128)(2,1)S(1)}, u32[]{:S(2)}, u32[]{:S(2)}) collective-permute-start(bf16[1,256,2,128]{3,1,2,0:T(8,128)(2,1)S(1)} %bitcast.262), channel_id=1, source_target_pairs={{0,256},{32,288},{64,320},{96,352},{128,384},{160,416},{192,448},{... | collective-permute-start | bytes 393224 | tf_op jit(solution)/shard_map/ppermute | solution.py:16
  80.0 1.4 %copy-start = (bf16[9,1,2,256,256]{3,4,2,1,0:T(8,128)(2,1)}, bf16[9,1,2,256,256]{3,4,2,1,0:T(8,128)(2,1)S(1)}, u32[]{:S(2)}) copy-start(bf16[9,1,2,256,256]{3,4,2,1,0:T(8,128)(2,1)S(1)} %fusion.10) | copy-start | bytes 7077892
where the time goes:
time: 90.4 us; the launch traced here: 89.8 us
  starting transfers between devices  47.8 us (53%)
  waiting for transfers between devices  19.9 us (22%)
  local copies, waits for them, and re-layouts  15.6 us (17%)
  matrix products  3.73 us (4%)
  other arithmetic  2.26 us (2%)
    ppermute x8, starting transfers between devices, shifted(): lax.ppermute(x, axis, [(i, (i + by) % length) for i in range(length)])  29.3 us
    all_to_all x1, starting transfers between devices, per_device(): lax.all_to_all(local_spectra, 'dev', split_axis=0, concat_axis=1, tiled=T...  18.5 us
    all_to_all x1, waiting for transfers between devices, per_device(): lax.all_to_all(local_spectra, 'dev', split_axis=0, concat_axis=1, tiled=T...  16.3 us
    unnamed x10, local copies, waits for them, and re-layouts  5.1 us
    select_n x1, local copies, waits for them, and re-layouts, per_device(): return jnp.take(stacked, plan[0], axis=0)[None]  4.26 us
    ppermute x8, waiting for transfers between devices, shifted(): lax.ppermute(x, axis, [(i, (i + by) % length) for i in range(length)])  3.6 us
    gather x1, local copies, waits for them, and re-layouts, per_device(): return jnp.take(stacked, plan[0], axis=0)[None]  2.36 us
    dot_general x9, matrix products, correlate(): jnp.einsum('gzi,gkvi->gkzv', left_spectrum_rows, right_spectrum_rows, pre...  2.35 us
  transfers between devices with their start and end apart: 9, of which 3 were waited for; matrix products, arithmetic and copies ran while one was open for 1% of the time, Pallas kernels for 0%

commit v1 on v0

v1 whole, which is shorter than its diff:
```python
import math

import jax
import jax.numpy as jnp
import numpy as np
from jax import lax
from jax.experimental import pallas as pl
from jax.experimental.pallas import tpu as pltpu
from jax.sharding import Mesh, PartitionSpec as P

F = 32
TAPS = 4
SPECTRA = 128
FRAMES = 131
HERE = 8
LANES = 128
TILES = 33
BLOCK = (32, 2, HERE, SPECTRA)


def dft_table():
    f = np.arange(F)[:, None]
    n = np.arange(F)[None, :]
    angle = 2.0 * math.pi * ((f * n) % F) / F
    cosine = np.tile(np.cos(angle), (1, TAPS))
    sine = np.tile(np.sin(angle), (1, TAPS))
    real_rows = np.concatenate([cosine, sine], axis=1)
    imag_rows = np.concatenate([-sine, cosine], axis=1)
    return np.concatenate([real_rows, imag_rows], axis=0).astype(np.float32)


def split(x):
    high = x.astype(jnp.bfloat16)
    low = (x - high.astype(jnp.float32)).astype(jnp.bfloat16)
    return high, low


def nt(a, b):
    return lax.dot_general(a, b, (((1,), (1,)), ((), ())), preferred_element_type=jnp.float32)


def spectra_kernel(v_ref, taps_ref, table_ref, out_ref, rows, placed):
    for c in range(2):
        for q in range(TILES - 1):
            rows[c, q * HERE : (q + 1) * HERE, :] = v_ref[c, :, q * LANES : (q + 1) * LANES]
        rows[c, (TILES - 1) * HERE :, : FRAMES * F - (TILES - 1) * LANES] = v_ref[
            c, :, (TILES - 1) * LANES :
        ]
    taps = taps_ref[...]
    tap_row = jnp.concatenate([taps[p : p + 1, :] for p in range(TAPS)], axis=1)
    weights = table_ref[...] * jnp.concatenate([tap_row, tap_row], axis=1)
    w_high, w_low = split(weights)
    w_both = jnp.concatenate([w_high, w_low], axis=0)
    lane = lax.broadcasted_iota(jnp.int32, (F, LANES), 1)
    for i in range(HERE):
        halves = []
        for c in range(2):
            here = rows[c, pl.ds(i, 32, stride=HERE), :]
            after = rows[c, pl.ds(i + HERE, 32, stride=HERE), :]
            parts = [here]
            for j in range(1, 4):
                parts.append(pltpu.roll(jnp.where(lane < F * j, after, here), LANES - F * j, 1))
            halves.append(jnp.concatenate(parts, axis=0))
        x_high, x_low = split(jnp.concatenate(halves, axis=1))
        both = nt(w_both, x_high)
        result = both[: 2 * F] + both[2 * F :] + nt(w_high, x_low)
        placed[pl.ds(i, F, stride=2 * HERE), :] = result[:F]
        placed[pl.ds(HERE + i, F, stride=2 * HERE), :] = result[F:]
    values = placed[...].astype(jnp.bfloat16).reshape(2, 16, 2, HERE, SPECTRA)
    out_ref[:, 0] = values[0]
    out_ref[:, 1] = values[1]


def compute_spectra(voltage, filter_taps):
    return pl.pallas_call(
        spectra_kernel,
        out_shape=jax.ShapeDtypeStruct((16, 2, 2, HERE, SPECTRA), jnp.bfloat16),
        in_specs=[pl.BlockSpec(memory_space=pltpu.VMEM)] * 3,
        out_specs=pl.BlockSpec(memory_space=pltpu.VMEM),
        scratch_shapes=[
            pltpu.VMEM((2, TILES * HERE, LANES), jnp.float32),
            pltpu.VMEM((F * 2 * HERE, SPECTRA), jnp.float32),
        ],
        cost_estimate=pl.CostEstimate(flops=10**8, bytes_accessed=400000, transcendentals=0),
        name="spectra",
    )(voltage, filter_taps, jnp.asarray(dft_table()))


def correlate_kernel(count, first, slots_ref, own_ref, partners_ref, *rest):
    out_ref, staged, sems = rest[-3:]
    own = own_ref[...]
    left = jnp.concatenate(
        [own[:, 0].reshape(256, SPECTRA), own[:, 1].reshape(256, SPECTRA)], axis=1
    )
    copies = []
    for b in range(count):
        real_part = partners_ref[b, :, 0].reshape(256, SPECTRA)
        imag_part = partners_ref[b, :, 1].reshape(256, SPECTRA)
        scale = 1.0 / SPECTRA
        staged[b, 0] = (
            nt(left, jnp.concatenate([real_part, imag_part], axis=1)) * scale
        ).astype(jnp.bfloat16)
        staged[b, 1] = (
            nt(left, jnp.concatenate([-imag_part, real_part], axis=1)) * scale
        ).astype(jnp.bfloat16)
        copy = pltpu.make_async_copy(staged.at[b], out_ref.at[slots_ref[first + b]], sems.at[b])
        copy.start()
        copies.append(copy)
    for copy in copies:
        copy.wait()


def correlate(slots, first, own, partners, before=None):
    count = partners.shape[0]
    operands = [slots, own, partners]
    in_specs = [
        pl.BlockSpec(memory_space=pltpu.SMEM),
        pl.BlockSpec(memory_space=pltpu.VMEM),
        pl.BlockSpec(memory_space=pltpu.VMEM),
    ]
    aliases = {}
    if before is not None:
        operands.append(before)
        in_specs.append(pl.BlockSpec(memory_space=pl.ANY))
        aliases = {3: 0}

    def kernel(*refs):
        correlate_kernel(count, first, *refs)

    return pl.pallas_call(
        kernel,
        out_shape=jax.ShapeDtypeStruct((9, 2, 256, 256), jnp.bfloat16),
        in_specs=in_specs,
        out_specs=pl.BlockSpec(memory_space=pl.ANY),
        scratch_shapes=[
            pltpu.VMEM((count, 2, 256, 256), jnp.bfloat16),
            pltpu.SemaphoreType.DMA((count,)),
        ],
        input_output_aliases=aliases,
        cost_estimate=pl.CostEstimate(
            flops=count * 2**26, bytes_accessed=count * 400000, transcendentals=0
        ),
        name="correlate",
    )(*operands)


def per_device(voltage, filter_taps, plan):
    x_lo, y, core = lax.axis_index("x_lo"), lax.axis_index("y"), lax.axis_index("core")
    spectra = compute_spectra(voltage, filter_taps)

    rows = jnp.arange(4, dtype=jnp.int32)
    steps = (y - rows) % 4
    other_core = jnp.where(core == 0, jnp.where(steps == 0, 7, 2 * steps - 1), 2 * steps + 1)
    others = (y - jnp.arange(1, 4, dtype=jnp.int32)) % 4
    distances = jnp.concatenate(
        [jnp.array([0, 8, 2, 4, 6], jnp.int32), other_core]
    )
    slots = jnp.sum(
        jnp.where(
            plan[0][None, :] == distances[:, None], jnp.arange(9, dtype=jnp.int32)[None, :], 0
        ),
        axis=1,
    )

    by_z = lax.all_to_all(spectra, "z", split_axis=0, concat_axis=0, tiled=True)
    by_x_hi = jnp.moveaxis(by_z, 1, 0)
    to_x = jnp.stack([by_x_hi, by_x_hi]).reshape(4, *by_x_hi.shape[1:])
    along_x = lax.all_to_all(to_x, ("x_lo", "x_hi"), split_axis=0, concat_axis=0, tiled=True)
    pair = along_x.reshape(2, *BLOCK)
    own = lax.dynamic_index_in_dim(pair, x_lo, 0, keepdims=False)
    across = lax.dynamic_index_in_dim(pair, 1 - x_lo, 0, keepdims=False)

    own_there = (rows > y) | ((rows == y) & (core == 0))
    to_y = jnp.where(own_there[:, None, None, None, None], own[None], across[None])
    along_y = lax.all_to_all(to_y, "y", split_axis=0, concat_axis=0, tiled=True)
    out = correlate(slots, 0, own, jnp.stack([own, across]))

    swapped = lax.ppermute(along_y, "core", [(0, 1), (1, 0)])
    out = correlate(slots, 2, own, along_y[others], out)
    out = correlate(slots, 5, own, swapped, out)
    return out[None, :, None]


def solution(mesh):
    fine = Mesh(mesh.devices.reshape(2, 4, 2, 2, 16), ("x_lo", "y", "core", "x_hi", "z"))
    grp, dev = ("x_lo", "y", "core"), ("x_hi", "z")
    return jax.shard_map(
        per_device,
        mesh=fine,
        in_specs=(P(None, grp + dev, None), P(), P(grp, None)),
        out_specs=P(grp, None, dev, None, None, None),
        check_vma=False,
    )
```

time: 90.4 us -> 71.5 us (0.79)
  starting transfers between devices: 47.8 us -> 16.7 us
  blocking collectives: 0 us -> 27.7 us
  local copies, waits for them, and re-layouts: 15.6 us -> 2.88 us
  Pallas kernels: 0 us -> 9.01 us
  waiting for transfers between devices: 19.9 us -> 12.2 us
  matrix products: 3.73 us -> 0 us
    all_to_all x0 -> x1, blocking collectives: none -> 27.7 us  [per_device(): by_z = lax.all_to_all(spectra, 'z', split_axis=0, concat_axis=0, tiled=True)]
    ppermute x8 -> x1, starting transfers between devices: 29.3 us -> 8.53 us  [per_device(): swapped = lax.ppermute(along_y, 'core', [(0, 1), (1, 0)])]
    all_to_all x1 -> x2, starting transfers between devices: 18.5 us -> 8.18 us  [the longest x1 4.18 us: per_device(): along_y = lax.all_to_all(to_y, 'y', split_axis=0, concat_axis=0, tiled=True)]
    pallas_call x0 -> x4, Pallas kernels: none -> 9.01 us  [the longest x3 6.73 us: correlate(): pl.pallas_call(kernel, out_shape=jax.ShapeDtypeStruct((9, 2, 256, 256), j...]
    unnamed x10 -> x8, local copies, waits for them, and re-layouts: 5.1 us -> 0.79 us
    select_n x1 -> x0, local copies, waits for them, and re-layouts: 4.26 us -> none  [per_device(): return jnp.take(stacked, plan[0], axis=0)[None]]
    all_to_all x1 -> x2, waiting for transfers between devices: 16.3 us -> 12.1 us  [the longest x1 6.92 us: per_device(): along_y = lax.all_to_all(to_y, 'y', split_axis=0, concat_axis=0, tiled=True)]
    dot_general x13 -> x0, matrix products: 3.73 us -> none  [the longest x9 2.35 us: correlate(): jnp.einsum('gzi,gkvi->gkzv', left_spectrum_rows, right_spectrum_rows, pre...]
  transfers between devices with their start and end apart: 9 -> 3, of which waited for: 3 -> 2; matrix products, arithmetic and copies ran while one was open for 1% -> 4% of each run, Pallas kernels for 0% -> 6%
where the time goes in v1:
time: 71.5 us; the launch traced here: 71.1 us
  blocking collectives  27.7 us (39%)
  starting transfers between devices  16.7 us (23%)
  waiting for transfers between devices  12.2 us (17%)
  Pallas kernels  9.01 us (13%)
  local copies, waits for them, and re-layouts  2.88 us (4%)
  other arithmetic  2.51 us (4%)
    all_to_all x1, blocking collectives, per_device(): by_z = lax.all_to_all(spectra, 'z', split_axis=0, concat_axis=0, tiled=True)  27.7 us
    ppermute x1, starting transfers between devices, per_device(): swapped = lax.ppermute(along_y, 'core', [(0, 1), (1, 0)])  8.53 us
    all_to_all x1, waiting for transfers between devices, per_device(): along_y = lax.all_to_all(to_y, 'y', split_axis=0, concat_axis=0, tiled=True)  6.92 us
    pallas_call x3, Pallas kernels, correlate(): pl.pallas_call(kernel, out_shape=jax.ShapeDtypeStruct((9, 2, 256, 256), j...  6.73 us
    all_to_all x1, waiting for transfers between devices, per_device(): lax.all_to_all(to_x, ('x_lo', 'x_hi'), split_axis=0, concat_axis=0, tiled...  5.23 us
    all_to_all x1, starting transfers between devices, per_device(): along_y = lax.all_to_all(to_y, 'y', split_axis=0, concat_axis=0, tiled=True)  4.18 us
    all_to_all x1, starting transfers between devices, per_device(): lax.all_to_all(to_x, ('x_lo', 'x_hi'), split_axis=0, concat_axis=0, tiled...  4 us
    pallas_call x1, Pallas kernels, compute_spectra(): pl.pallas_call(spectra_kernel, out_shape=jax.ShapeDtypeStruct((16, 2, 2,...  2.28 us
  transfers between devices with their start and end apart: 3, of which 2 were waited for; matrix products, arithmetic and copies ran while one was open for 4% of the time, Pallas kernels for 6%

profile of v1, /device:TPU:1, one launch (start us, length us, event | category | flops | bytes accessed | tf_op | source)
XLA Modules:
  0.0 71.1 jit_solution(13625780571485326635)
XLA Ops:
  0.0 0.0 copy-start.3
  0.0 0.0 copy-start.2
  0.0 2.3 %spectra.1 = bf16[16,2,2,8,128]{4,3,2,1,0:T(8,128)(2,1)} custom-call(f32[2,8,4192]{2,1,0:T(8,128)} %v_ref.1, f32[4,32]{1,0:T(4,128)} %taps_ref.1, f32[64,256]{1,0:T(8,128)} %constant.64.clone.table_ref), custom_call_target="tpu_custom_call" | custom-call | flops 100000000 | bytes 400000 | tf_op jit(solution)/shard_map/spectra/pallas_call | solution.py:75
  2.3 27.7 %all_to_all.15 = bf16[16,2,2,8,128]{4,3,2,1,0:T(8,128)(2,1)S(1)} all-to-all(bf16[16,2,2,8,128]{4,3,2,1,0:T(8,128)(2,1)} %spectra.1), channel_id=1, replica_groups=mesh['x_lo'=2,'y'=4,'core'=2,'x_hi'=2,'z'=16] {'z'}, dimensions={0} | all-to-all | bytes 262144 | tf_op jit(solution)/shard_map/all_to_all | solution.py:165
  30.0 0.7 %copy.11 = bf16[2,2,16,2,8,128]{5,4,3,2,1,0:T(8,128)(2,1)} copy(bf16[2,2,16,2,8,128]{5,4,3,1,2,0:T(8,128)(2,1)S(1)} %pad_maximum_fusion) | data formatting | bytes 524288 | tf_op jit(solution)/shard_map/stack | solution.py:167
  30.8 4.0 %all-to-all-start.1 = ((bf16[4,16,2,8,128]{4,3,2,1,0:T(8,128)(2,1)}), bf16[4,16,2,8,128]{4,3,2,1,0:T(8,128)(2,1)S(1)}, u32[]{:S(2)}, u32[]{:S(2)}) async-start(bf16[4,16,2,8,128]{4,3,2,1,0:T(8,128)(2,1)} %bitcast.3), calls=%async_computation.1 | async-start | bytes 524288 | tf_op jit(solution)/shard_map/all_to_all | solution.py:168
  34.8 5.2 %all-to-all-done.1 = bf16[4,16,2,8,128]{4,3,2,1,0:T(8,128)(2,1)S(1)} async-done(((bf16[4,16,2,8,128]{4,3,2,1,0:T(8,128)(2,1)}), bf16[4,16,2,8,128]{4,3,2,1,0:T(8,128)(2,1)S(1)}, u32[]{:S(2)}, u32[]{:S(2)}) %all-to-all-start.1) | async-done | bytes 262176 | tf_op jit(solution)/shard_map/all_to_all | solution.py:168
  40.0 0.0 copy-start
  40.0 0.9 %broadcast_select_fusion = bf16[4,32,2,8,128]{4,3,2,1,0:T(8,128)(2,1)} fusion(pred[4]{0:T(512)(128)(4,1)S(1)} %and_or_fusion, bf16[32,2,8,128]{3,2,1,0:T(8,128)(2,1)S(1)} %bitcast.17, bf16[32,2,8,128]{3,2,1,0:T(8,128)(2,1)S(1)} %bitcast.13), kind=kLoop, calls=%fused_computation.1 | loop fusion | flops 262144 | bytes 786436 | tf_op jit(solution)/shard_map/jit(_where)/select_n | solution.py:174
  40.9 4.2 %all-to-all-start.2 = ((bf16[4,32,2,8,128]{4,3,2,1,0:T(8,128)(2,1)}), bf16[4,32,2,8,128]{4,3,2,1,0:T(8,128)(2,1)S(1)}, u32[]{:S(2)}, u32[]{:S(2)}) async-start(bf16[4,32,2,8,128]{4,3,2,1,0:T(8,128)(2,1)} %broadcast_select_fusion), calls=%async_computation.2 | async-start | bytes 1048576 | tf_op jit(solution)/shard_map/all_to_all | solution.py:175
  45.1 6.9 %all-to-all-done.2 = bf16[4,32,2,8,128]{4,3,2,1,0:T(8,128)(2,1)S(1)} async-done(((bf16[4,32,2,8,128]{4,3,2,1,0:T(8,128)(2,1)}), bf16[4,32,2,8,128]{4,3,2,1,0:T(8,128)(2,1)S(1)}, u32[]{:S(2)}, u32[]{:S(2)}) %all-to-all-start.2) | async-done | bytes 524320 | tf_op jit(solution)/shard_map/all_to_all | solution.py:175
  52.0 8.5 %collective-permute-start = (bf16[4,32,2,8,128]{4,3,2,1,0:T(8,128)(2,1)S(1)}, bf16[4,32,2,8,128]{4,3,2,1,0:T(8,128)(2,1)S(1)}, u32[]{:S(2)}, u32[]{:S(2)}) collective-permute-start(bf16[4,32,2,8,128]{4,3,2,1,0:T(8,128)(2,1)S(1)} %all-to-all-done.2), channel_id=1, source_target_pairs={{0,32},{32,0},{1,33},{33,1},{2,34},{34,2},{3,35},{35,3},{4,36},{36... | collective-permute-start | bytes 1572872 | tf_op jit(solution)/shard_map/ppermute | solution.py:178
  60.6 0.0 copy-done.3
  60.6 0.1 pad_add_fusion
  60.7 0.0 copy-done.2
  60.7 0.8 %select_reduce_fusion.refs_0_ = s32[9]{0:T(128)} fusion(s32[9]{0:T(128)S(1)} %bitcast.20, s32[9]{0:T(128)S(1)} %pad_add_fusion), kind=kLoop, calls=%fused_computation.4 | loop fusion | flops 234 | bytes 108 | tf_op jit(solution)/shard_map/reduce_sum | solution.py:158
  61.4 0.7 %pad_maximum_fusion.1.refs_2_ = bf16[2,32,2,8,128]{4,3,2,1,0:T(8,128)(2,1)} fusion(bf16[1,32,2,8,128]{4,3,2,1,0:T(8,128)(2,1)S(1)} %get-tuple-element.5, bf16[1,32,2,8,128]{4,3,2,1,0:T(8,128)(2,1)S(1)} %get-tuple-element.6), kind=kLoop, calls=%fused_computation.3 | loop fusion | flops 131072 | bytes 524288 | tf_op jit(solution)/shard_map/stack | solution.py:176
  62.2 0.0 copy-done
  62.2 2.1 %correlate.3.refs_3_ = bf16[9,2,256,256]{3,2,1,0:T(8,128)(2,1)} custom-call(s32[9]{0:T(128)} %select_reduce_fusion.refs_0_, bf16[32,2,8,128]{3,2,1,0:T(8,128)(2,1)} %bitcast.14, bf16[2,32,2,8,128]{4,3,2,1,0:T(8,128)(2,1)} %pad_maximum_fusion.1.refs_2_), custom_call_target="tpu_custom_call" | custom-call | flops 134217728 | bytes 800000 | tf_op jit(solution)/shard_map/correlate/pallas_call | solution.py:130
  64.3 1.4 %gather_fusion = bf16[3,32,2,8,128]{4,3,2,1,0:T(8,128)(2,1)} fusion(bf16[4,32,2,8,128]{4,3,2,1,0:T(8,128)(2,1)S(1)} %all-to-all-done.2, s32[1024]{0:T(1024)S(1)} %pad_clamp_fusion), kind=kCustom, calls=%fused_computation | custom fusion | bytes 786444 | tf_op jit(solution)/shard_map/gather | solution.py:179
  65.6 2.2 %correlate.4.refs_3_ = bf16[9,2,256,256]{3,2,1,0:T(8,128)(2,1)} custom-call(s32[9]{0:T(128)} %select_reduce_fusion.refs_0_, bf16[32,2,8,128]{3,2,1,0:T(8,128)(2,1)} %bitcast.15, bf16[3,32,2,8,128]{4,3,2,1,0:T(8,128)(2,1)} %gather_fusion, bf16[9,2,256,256]{3,2,1,0:T(8,128)(2,1)} %correlate.3.refs_3_), custom_call_target="tpu_custom_call", output_to_operand_aliasing={{}: (3, {})} | custom-call | flops 201326592 | bytes 1200000 | tf_op jit(solution)/shard_map/correlate/pallas_call | solution.py:130
  67.9 0.0 collective-permute-done.refs_2_
  67.9 0.0 copy-start.1
  67.9 0.8 %copy-done.1 = bf16[4,32,2,8,128]{4,3,2,1,0:T(8,128)(2,1)} copy-done((bf16[4,32,2,8,128]{4,3,2,1,0:T(8,128)(2,1)}, bf16[4,32,2,8,128]{4,3,2,1,0:T(8,128)(2,1)S(1)}, u32[]{:S(2)}) %copy-start.1) | copy-done | bytes 524312
  68.7 2.4 %correlate.5 = bf16[9,2,256,256]{3,2,1,0:T(8,128)(2,1)} custom-call(s32[9]{0:T(128)} %select_reduce_fusion.refs_0_, bf16[32,2,8,128]{3,2,1,0:T(8,128)(2,1)} %bitcast.16, bf16[4,32,2,8,128]{4,3,2,1,0:T(8,128)(2,1)} %copy-done.1, bf16[9,2,256,256]{3,2,1,0:T(8,128)(2,1)} %correlate.4.refs_3_), custom_call_target="tpu_custom_call", output_to_operand_aliasing={{}: (3, {})} | custom-call | flops 268435456 | bytes 1600000 | tf_op jit(solution)/shard_map/correlate/pallas_call | solution.py:130
  (6 shorter events, 0.1 us)
Async XLA Ops:
  0.0 60.6 %copy-start.3 = (s32[5]{0:T(128)S(1)}, s32[5]{0:T(128)}, u32[]{:S(2)}) copy-start(s32[5]{0:T(128)} %constant.65.clone) | copy-start | bytes 64
  0.0 60.7 %copy-start.2 = (s32[1,9]{1,0:T(1,128)S(1)}, s32[1,9]{1,0:T(1,128)}, u32[]{:S(2)}) copy-start(s32[1,9]{1,0:T(1,128)} %param.7) | copy-start | bytes 112
  30.8 9.2 %all-to-all-start.1 = ((bf16[4,16,2,8,128]{4,3,2,1,0:T(8,128)(2,1)}), bf16[4,16,2,8,128]{4,3,2,1,0:T(8,128)(2,1)S(1)}, u32[]{:S(2)}, u32[]{:S(2)}) async-start(bf16[4,16,2,8,128]{4,3,2,1,0:T(8,128)(2,1)} %bitcast.3), calls=%async_computation.1 | async-start | bytes 524288 | tf_op jit(solution)/shard_map/all_to_all | solution.py:168
  40.0 22.2 %copy-start = (bf16[1,32,2,8,128]{4,3,2,1,0:T(8,128)(2,1)}, bf16[1,32,2,8,128]{4,3,2,1,0:T(8,128)(2,1)S(1)}, u32[]{:S(2)}) copy-start(bf16[1,32,2,8,128]{4,3,2,1,0:T(8,128)(2,1)S(1)} %get-tuple-element.6) | copy-start | bytes 393220
  40.9 11.1 %all-to-all-start.2 = ((bf16[4,32,2,8,128]{4,3,2,1,0:T(8,128)(2,1)}), bf16[4,32,2,8,128]{4,3,2,1,0:T(8,128)(2,1)S(1)}, u32[]{:S(2)}, u32[]{:S(2)}) async-start(bf16[4,32,2,8,128]{4,3,2,1,0:T(8,128)(2,1)} %broadcast_select_fusion), calls=%async_computation.2 | async-start | bytes 1048576 | tf_op jit(solution)/shard_map/all_to_all | solution.py:175
  52.0 15.8 %collective-permute-start = (bf16[4,32,2,8,128]{4,3,2,1,0:T(8,128)(2,1)S(1)}, bf16[4,32,2,8,128]{4,3,2,1,0:T(8,128)(2,1)S(1)}, u32[]{:S(2)}, u32[]{:S(2)}) collective-permute-start(bf16[4,32,2,8,128]{4,3,2,1,0:T(8,128)(2,1)S(1)} %all-to-all-done.2), channel_id=1, source_target_pairs={{0,32},{32,0},{1,33},{33,1},{2,34},{34,2},{3,35},{35,3},{4,36},{36... | collective-permute-start | bytes 1572872 | tf_op jit(solution)/shard_map/ppermute | solution.py:178
  67.9 0.8 %copy-start.1 = (bf16[4,32,2,8,128]{4,3,2,1,0:T(8,128)(2,1)}, bf16[4,32,2,8,128]{4,3,2,1,0:T(8,128)(2,1)S(1)}, u32[]{:S(2)}) copy-start(bf16[4,32,2,8,128]{4,3,2,1,0:T(8,128)(2,1)S(1)} %collective-permute-done.refs_2_) | copy-start | bytes 1572868

commit v2 on v1

v2 whole, which is shorter than its diff:
```python
import math

import jax
import jax.numpy as jnp
import numpy as np
from jax import lax
from jax.experimental import pallas as pl
from jax.experimental.pallas import tpu as pltpu
from jax.sharding import PartitionSpec as P

F = 32
TAPS = 4
SPECTRA = 128
FRAMES = 131
HERE = 8
LANES = 128
TILES = 33
ROUNDS = 9
BLK = 256
BLOCK = (32, 2, HERE, SPECTRA)


def dft_table():
    f = np.arange(F)[:, None]
    n = np.arange(F)[None, :]
    angle = 2.0 * math.pi * ((f * n) % F) / F
    cosine = np.tile(np.cos(angle), (1, TAPS))
    sine = np.tile(np.sin(angle), (1, TAPS))
    real_rows = np.concatenate([cosine, sine], axis=1)
    imag_rows = np.concatenate([-sine, cosine], axis=1)
    return np.concatenate([real_rows, imag_rows], axis=0).astype(np.float32)


def split(x):
    high = x.astype(jnp.bfloat16)
    low = (x - high.astype(jnp.float32)).astype(jnp.bfloat16)
    return high, low


def nt(a, b):
    return lax.dot_general(a, b, (((1,), (1,)), ((), ())), preferred_element_type=jnp.float32)


def spectra_kernel(v_ref, taps_ref, table_ref, out_ref, rows, placed):
    for c in range(2):
        for q in range(TILES - 1):
            rows[c, q * HERE : (q + 1) * HERE, :] = v_ref[c, :, q * LANES : (q + 1) * LANES]
        rows[c, (TILES - 1) * HERE :, : FRAMES * F - (TILES - 1) * LANES] = v_ref[
            c, :, (TILES - 1) * LANES :
        ]
    taps = taps_ref[...]
    tap_row = jnp.concatenate([taps[p : p + 1, :] for p in range(TAPS)], axis=1)
    weights = table_ref[...] * jnp.concatenate([tap_row, tap_row], axis=1)
    w_high, w_low = split(weights)
    w_both = jnp.concatenate([w_high, w_low], axis=0)
    lane = lax.broadcasted_iota(jnp.int32, (F, LANES), 1)
    for i in range(HERE):
        halves = []
        for c in range(2):
            here = rows[c, pl.ds(i, 32, stride=HERE), :]
            after = rows[c, pl.ds(i + HERE, 32, stride=HERE), :]
            parts = [here]
            for j in range(1, 4):
                parts.append(pltpu.roll(jnp.where(lane < F * j, after, here), LANES - F * j, 1))
            halves.append(jnp.concatenate(parts, axis=0))
        x_high, x_low = split(jnp.concatenate(halves, axis=1))
        both = nt(w_both, x_high)
        result = both[: 2 * F] + both[2 * F :] + nt(w_high, x_low)
        placed[pl.ds(i, F, stride=2 * HERE), :] = result[:F]
        placed[pl.ds(HERE + i, F, stride=2 * HERE), :] = result[F:]
    out_ref[...] = placed[...].astype(jnp.bfloat16).reshape(BLOCK)


def compute_spectra(voltage, filter_taps):
    return pl.pallas_call(
        spectra_kernel,
        out_shape=jax.ShapeDtypeStruct(BLOCK, jnp.bfloat16),
        in_specs=[pl.BlockSpec(memory_space=pltpu.VMEM)] * 3,
        out_specs=pl.BlockSpec(memory_space=pltpu.VMEM),
        scratch_shapes=[
            pltpu.VMEM((2, TILES * HERE, LANES), jnp.float32),
            pltpu.VMEM((F * 2 * HERE, SPECTRA), jnp.float32),
        ],
        cost_estimate=pl.CostEstimate(flops=10**8, bytes_accessed=400000, transcendentals=0),
        name="spectra",
    )(voltage, filter_taps, jnp.asarray(dft_table()))


def in_vmem(x):
    return pltpu.with_memory_space_constraint(x, pltpu.VMEM)


def correlate(plan, own, blocks, entries, before=None):
    count = len(entries)

    def kernel(plan_hbm, own_ref, *rest):
        block_refs, rest = rest[: len(blocks)], rest[len(blocks) :]
        out_ref, staged, plan_ref, plan_sem, sems = rest[-5:]
        fetch = pltpu.make_async_copy(plan_hbm, plan_ref, plan_sem)
        fetch.start()
        core = lax.axis_index("grp") % 2
        own = own_ref[...]
        left = jnp.concatenate(
            [own[:, 0].reshape(BLK, SPECTRA), own[:, 1].reshape(BLK, SPECTRA)], axis=1
        )
        copies = []
        for b, (array, index, distance, always) in enumerate(entries):
            ref = block_refs[array]
            real_part = ref[index, :, 0].reshape(BLK, SPECTRA)
            imag_part = ref[index, :, 1].reshape(BLK, SPECTRA)
            scale = 1.0 / SPECTRA
            staged[b, 0] = (
                nt(left, jnp.concatenate([real_part, imag_part], axis=1)) * scale
            ).astype(jnp.bfloat16)
            staged[b, 1] = (
                nt(left, jnp.concatenate([-imag_part, real_part], axis=1)) * scale
            ).astype(jnp.bfloat16)
            if b == 0:
                fetch.wait()
            wanted = distance(core)
            slot = jnp.int32(0)
            for r in range(ROUNDS):
                slot = jnp.where(plan_ref[0, r] == wanted, r, slot)
            copy = pltpu.make_async_copy(staged.at[b], out_ref.at[slot], sems.at[b])
            if always:
                copy.start()
            else:
                pl.when((wanted >= 0) & (wanted < ROUNDS))(copy.start)
            copies.append((copy, always, wanted))
        for copy, always, wanted in copies:
            if always:
                copy.wait()
            else:
                pl.when((wanted >= 0) & (wanted < ROUNDS))(copy.wait)

    operands = [plan, in_vmem(own), *[in_vmem(b) for b in blocks]]
    in_specs = [pl.BlockSpec(memory_space=pl.ANY)] + [pl.BlockSpec(memory_space=pltpu.VMEM)] * (
        1 + len(blocks)
    )
    aliases = {}
    if before is not None:
        aliases = {len(operands): 0}
        operands.append(before)
        in_specs.append(pl.BlockSpec(memory_space=pl.ANY))
    return pl.pallas_call(
        kernel,
        out_shape=jax.ShapeDtypeStruct((ROUNDS, 2, BLK, BLK), jnp.bfloat16),
        in_specs=in_specs,
        out_specs=pl.BlockSpec(memory_space=pl.ANY),
        scratch_shapes=[
            pltpu.VMEM((count, 2, BLK, BLK), jnp.bfloat16),
            pltpu.SMEM((1, ROUNDS), jnp.int32),
            pltpu.SemaphoreType.DMA,
            pltpu.SemaphoreType.DMA((count,)),
        ],
        input_output_aliases=aliases,
        cost_estimate=pl.CostEstimate(
            flops=count * 2**26, bytes_accessed=count * 400000, transcendentals=0
        ),
        name="correlate",
    )(*operands)


def per_device(voltage, filter_taps, plan):
    core = lax.axis_index("grp") % 2
    spectra = compute_spectra(voltage, filter_taps)
    own = lax.all_to_all(spectra, "dev", split_axis=0, concat_axis=0, tiled=True)

    def fetch(x, back):
        return lax.ppermute(
            x,
            "grp",
            [((2 * (chip - back - c)) % 16 + c, 2 * chip + c) for chip in range(8) for c in range(2)],
        )

    def swap(x):
        return lax.ppermute(x, "grp", [(g, g ^ 1) for g in range(16)])

    other = swap(own)
    pair = jnp.where(core == 0, jnp.stack([own, other]), jnp.stack([other, own]))
    near = fetch(pair, 1)
    far = fetch(pair, 3)
    near_swapped = swap(near)
    far_swapped = swap(far)

    def here(back, c):
        return lambda core: 2 * (back + core) + core - c

    def there(back, c):
        return lambda core: 2 * (back + 1 - core) + core - c

    out = correlate(
        plan, own, [pair], [(0, 0, lambda core: core, False), (0, 1, lambda core: core - 1, False)]
    )
    out = correlate(
        plan,
        own,
        [near, far],
        [(0, 0, here(1, 0), True), (0, 1, here(1, 1), True), (1, 0, here(3, 0), False), (1, 1, here(3, 1), True)],
        out,
    )
    out = correlate(
        plan,
        own,
        [near_swapped, far_swapped],
        [(0, 0, there(1, 0), True), (0, 1, there(1, 1), True), (1, 0, there(3, 0), True), (1, 1, there(3, 1), True)],
        out,
    )
    return out[None, :, None]


def solution(mesh):
    return jax.shard_map(
        per_device,
        mesh=mesh,
        in_specs=(P(None, ("grp", "dev"), None), P(), P("grp", None)),
        out_specs=P("grp", None, "dev", None, None, None),
        check_vma=False,
    )
```

time: 71.5 us -> 67 us (0.937); the launches traced: 71.1 us -> 65.8 us
  waiting for transfers between devices: 12.2 us -> 4.88 us
  blocking collectives: 27.7 us -> 34.8 us
  local copies, waits for them, and re-layouts: 2.88 us -> 0 us
  other arithmetic: 2.51 us -> 0.03 us
  starting transfers between devices: 16.7 us -> 18.4 us
  Pallas kernels: 9.01 us -> 7.63 us
    all_to_all x2 -> x0, waiting for transfers between devices: 12.1 us -> none  [the longest x1 6.92 us: per_device(): along_y = lax.all_to_all(to_y, 'y', split_axis=0, concat_axis=0, tiled=True)]
    ppermute x1 -> x5, starting transfers between devices: 8.53 us -> 18.4 us  [the longest x3 11.3 us: swap(): return lax.ppermute(x, 'grp', [(g, g ^ 1) for g in range(16)])]
    all_to_all x2 -> x0, starting transfers between devices: 8.18 us -> none  [the longest x1 4.18 us: per_device(): along_y = lax.all_to_all(to_y, 'y', split_axis=0, concat_axis=0, tiled=True)]
    all_to_all x1, blocking collectives: 27.7 us -> 34.8 us  [per_device(): lax.all_to_all(spectra, 'dev', split_axis=0, concat_axis=0, tiled=True)]
    ppermute x1 -> x5, waiting for transfers between devices: 0.01 us -> 4.88 us  [the longest x2 3.92 us: fetch(): lax.ppermute(x, 'grp', [(2 * (chip - back - c) % 16 + c, 2 * chip + c) fo...]
    pallas_call x4, Pallas kernels: 9.01 us -> 7.63 us  [the longest x3 5.37 us: correlate(): pl.pallas_call(kernel, out_shape=jax.ShapeDtypeStruct((ROUNDS, 2, BLK, BL...]
    gather x1 -> x0, local copies, waits for them, and re-layouts: 1.35 us -> none  [per_device(): out = correlate(slots, 2, own, along_y[others], out)]
    select_n x3 -> x1, other arithmetic: 0.93 us -> 0.03 us  [per_device(): jnp.where(core == 0, jnp.stack([own, other]), jnp.stack([other, own]))]
  transfers between devices with their start and end apart: 3 -> 5, of which waited for: 2 -> 2; matrix products, arithmetic and copies ran while one was open for 4% -> 0% of each run, Pallas kernels for 6% -> 5%
where the time goes in v2:
time: 67 us; the launch traced here: 65.8 us
  blocking collectives  34.8 us (52%)
  starting transfers between devices  18.4 us (27%)
  Pallas kernels  7.63 us (11%)
  waiting for transfers between devices  4.88 us (7%)
    all_to_all x1, blocking collectives, per_device(): lax.all_to_all(spectra, 'dev', split_axis=0, concat_axis=0, tiled=True)  34.8 us
    ppermute x3, starting transfers between devices, swap(): return lax.ppermute(x, 'grp', [(g, g ^ 1) for g in range(16)])  11.3 us
    ppermute x2, starting transfers between devices, fetch(): lax.ppermute(x, 'grp', [(2 * (chip - back - c) % 16 + c, 2 * chip + c) fo...  7.04 us
    pallas_call x3, Pallas kernels, correlate(): pl.pallas_call(kernel, out_shape=jax.ShapeDtypeStruct((ROUNDS, 2, BLK, BL...  5.37 us
    ppermute x2, waiting for transfers between devices, fetch(): lax.ppermute(x, 'grp', [(2 * (chip - back - c) % 16 + c, 2 * chip + c) fo...  3.92 us
    pallas_call x1, Pallas kernels, compute_spectra(): pl.pallas_call(spectra_kernel, out_shape=jax.ShapeDtypeStruct(BLOCK, jnp....  2.26 us
  transfers between devices with their start and end apart: 5, of which 2 were waited for; matrix products, arithmetic and copies ran while one was open for 0% of the time, Pallas kernels for 5%

profile of v2, /device:TPU:1, one launch (start us, length us, event | category | flops | bytes accessed | tf_op | source)
XLA Modules:
  0.0 65.8 jit_solution(18188385215719891076)
XLA Ops:
  0.0 2.3 %spectra.1 = bf16[32,2,8,128]{3,2,1,0:T(8,128)(2,1)} custom-call(f32[2,8,4192]{2,1,0:T(8,128)} %v_ref.1, f32[4,32]{1,0:T(4,128)} %taps_ref.1, f32[64,256]{1,0:T(8,128)} %constant.22.clone.table_ref), custom_call_target="tpu_custom_call" | custom-call | flops 100000000 | bytes 400000 | tf_op jit(solution)/shard_map/spectra/pallas_call | solution.py:75
  2.3 34.8 %all_to_all.5.own_ref = bf16[32,2,8,128]{3,2,1,0:T(8,128)(2,1)S(1)} all-to-all(bf16[32,2,8,128]{3,2,1,0:T(8,128)(2,1)} %spectra.1), channel_id=1, replica_groups=mesh['grp'=16,'dev'=32] {'dev'}, dimensions={0} | all-to-all | bytes 262144 | tf_op jit(solution)/shard_map/all_to_all | solution.py:167
  37.1 4.9 %collective-permute-start = (bf16[32,2,8,128]{3,2,1,0:T(8,128)(2,1)S(1)}, bf16[32,2,8,128]{3,2,1,0:T(8,128)(2,1)S(1)}, u32[]{:S(2)}, u32[]{:S(2)}) collective-permute-start(bf16[32,2,8,128]{3,2,1,0:T(8,128)(2,1)S(1)} %all_to_all.5.own_ref), channel_id=1, source_target_pairs={{0,32},{32,0},{64,96},{96,64},{128,160},{160,128},{192,224},{224,1... | collective-permute-start | bytes 393224 | tf_op jit(solution)/shard_map/ppermute | solution.py:177
  42.0 1.0 %collective-permute-done = bf16[32,2,8,128]{3,2,1,0:T(8,128)(2,1)S(1)} collective-permute-done((bf16[32,2,8,128]{3,2,1,0:T(8,128)(2,1)S(1)}, bf16[32,2,8,128]{3,2,1,0:T(8,128)(2,1)S(1)}, u32[]{:S(2)}, u32[]{:S(2)}) %collective-permute-start) | collective-permute-done | bytes 131104 | tf_op jit(solution)/shard_map/ppermute | solution.py:177
  42.9 4.8 %collective-permute-start.1 = (bf16[2,32,2,8,128]{4,3,2,1,0:T(8,128)(2,1)S(1)}, bf16[2,32,2,8,128]{4,3,2,1,0:T(8,128)(2,1)S(1)}, u32[]{:S(2)}, u32[]{:S(2)}) collective-permute-start(bf16[2,32,2,8,128]{4,3,2,1,0:T(8,128)(2,1)S(1)} %maximum_select_fusion.rest_0_), channel_id=1, source_target_pairs={{448,0},{416,32},{0,64},{480,96},{64,128},{32,160},{128,192},{96,2... | collective-permute-start | bytes 786440 | tf_op jit(solution)/shard_map/ppermute | solution.py:170
  47.8 2.2 %collective-permute-start.3 = (bf16[2,32,2,8,128]{4,3,2,1,0:T(8,128)(2,1)S(1)}, bf16[2,32,2,8,128]{4,3,2,1,0:T(8,128)(2,1)S(1)}, u32[]{:S(2)}, u32[]{:S(2)}) collective-permute-start(bf16[2,32,2,8,128]{4,3,2,1,0:T(8,128)(2,1)S(1)} %maximum_select_fusion.rest_0_), channel_id=1, source_target_pairs={{320,0},{288,32},{384,64},{352,96},{448,128},{416,160},{0,192},{48... | collective-permute-start | bytes 786440 | tf_op jit(solution)/shard_map/ppermute | solution.py:170
  50.0 3.9 %collective-permute-done.1.rest_0_ = bf16[2,32,2,8,128]{4,3,2,1,0:T(8,128)(2,1)S(1)} collective-permute-done((bf16[2,32,2,8,128]{4,3,2,1,0:T(8,128)(2,1)S(1)}, bf16[2,32,2,8,128]{4,3,2,1,0:T(8,128)(2,1)S(1)}, u32[]{:S(2)}, u32[]{:S(2)}) %collective-permute-start.1) | collective-permute-done | bytes 262176 | tf_op jit(solution)/shard_map/ppermute | solution.py:170
  53.9 4.3 %collective-permute-start.2 = (bf16[2,32,2,8,128]{4,3,2,1,0:T(8,128)(2,1)S(1)}, bf16[2,32,2,8,128]{4,3,2,1,0:T(8,128)(2,1)S(1)}, u32[]{:S(2)}, u32[]{:S(2)}) collective-permute-start(bf16[2,32,2,8,128]{4,3,2,1,0:T(8,128)(2,1)S(1)} %collective-permute-done.1.rest_0_), channel_id=1, source_target_pairs={{0,32},{32,0},{64,96},{96,64},{128,160},{160,128},{192,224},{224,1... | collective-permute-start | bytes 786440 | tf_op jit(solution)/shard_map/ppermute | solution.py:177
  58.2 0.0 collective-permute-done.3.rest_1_
  58.2 2.2 %collective-permute-start.4 = (bf16[2,32,2,8,128]{4,3,2,1,0:T(8,128)(2,1)S(1)}, bf16[2,32,2,8,128]{4,3,2,1,0:T(8,128)(2,1)S(1)}, u32[]{:S(2)}, u32[]{:S(2)}) collective-permute-start(bf16[2,32,2,8,128]{4,3,2,1,0:T(8,128)(2,1)S(1)} %collective-permute-done.3.rest_1_), channel_id=1, source_target_pairs={{0,32},{32,0},{64,96},{96,64},{128,160},{160,128},{192,224},{224,1... | collective-permute-start | bytes 786440 | tf_op jit(solution)/shard_map/ppermute | solution.py:177
  60.4 1.7 %correlate.3.rest_2_ = bf16[9,2,256,256]{3,2,1,0:T(8,128)(2,1)} custom-call(s32[1,9]{1,0:T(1,128)} %plan_hbm.5, bf16[32,2,8,128]{3,2,1,0:T(8,128)(2,1)S(1)} %all_to_all.5.own_ref, bf16[2,32,2,8,128]{4,3,2,1,0:T(8,128)(2,1)S(1)} %maximum_select_fusion.rest_0_), custom_call_target="tpu_custom_call" | custom-call | flops 134217728 | bytes 800000 | tf_op jit(solution)/shard_map/correlate/pallas_call | solution.py:145
  62.1 1.8 %correlate.4.rest_2_ = bf16[9,2,256,256]{3,2,1,0:T(8,128)(2,1)} custom-call(s32[1,9]{1,0:T(1,128)} %plan_hbm.5, bf16[32,2,8,128]{3,2,1,0:T(8,128)(2,1)S(1)} %all_to_all.5.own_ref, bf16[2,32,2,8,128]{4,3,2,1,0:T(8,128)(2,1)S(1)} %collective-permute-done.1.rest_0_, ...), custom_call_target="tpu_custom_call", output_to_operand_aliasing={{}: (4, {})} | custom-call | flops 268435456 | bytes 1600000 | tf_op jit(solution)/shard_map/correlate/pallas_call | solution.py:145
  63.9 0.0 collective-permute-done.2.rest_0_
  63.9 0.0 collective-permute-done.4.rest_1_
  63.9 1.9 %correlate.5 = bf16[9,2,256,256]{3,2,1,0:T(8,128)(2,1)} custom-call(s32[1,9]{1,0:T(1,128)} %plan_hbm.5, bf16[32,2,8,128]{3,2,1,0:T(8,128)(2,1)S(1)} %all_to_all.5.own_ref, bf16[2,32,2,8,128]{4,3,2,1,0:T(8,128)(2,1)S(1)} %collective-permute-done.2.rest_0_, ...), custom_call_target="tpu_custom_call", output_to_operand_aliasing={{}: (4, {})} | custom-call | flops 268435456 | bytes 1600000 | tf_op jit(solution)/shard_map/correlate/pallas_call | solution.py:145
  (1 shorter events, 0.0 us)
Async XLA Ops:
  37.1 5.9 %collective-permute-start = (bf16[32,2,8,128]{3,2,1,0:T(8,128)(2,1)S(1)}, bf16[32,2,8,128]{3,2,1,0:T(8,128)(2,1)S(1)}, u32[]{:S(2)}, u32[]{:S(2)}) collective-permute-start(bf16[32,2,8,128]{3,2,1,0:T(8,128)(2,1)S(1)} %all_to_all.5.own_ref), channel_id=1, source_target_pairs={{0,32},{32,0},{64,96},{96,64},{128,160},{160,128},{192,224},{224,1... | collective-permute-start | bytes 393224 | tf_op jit(solution)/shard_map/ppermute | solution.py:177
  42.9 11.0 %collective-permute-start.1 = (bf16[2,32,2,8,128]{4,3,2,1,0:T(8,128)(2,1)S(1)}, bf16[2,32,2,8,128]{4,3,2,1,0:T(8,128)(2,1)S(1)}, u32[]{:S(2)}, u32[]{:S(2)}) collective-permute-start(bf16[2,32,2,8,128]{4,3,2,1,0:T(8,128)(2,1)S(1)} %maximum_select_fusion.rest_0_), channel_id=1, source_target_pairs={{448,0},{416,32},{0,64},{480,96},{64,128},{32,160},{128,192},{96,2... | collective-permute-start | bytes 786440 | tf_op jit(solution)/shard_map/ppermute | solution.py:170
  47.8 10.4 %collective-permute-start.3 = (bf16[2,32,2,8,128]{4,3,2,1,0:T(8,128)(2,1)S(1)}, bf16[2,32,2,8,128]{4,3,2,1,0:T(8,128)(2,1)S(1)}, u32[]{:S(2)}, u32[]{:S(2)}) collective-permute-start(bf16[2,32,2,8,128]{4,3,2,1,0:T(8,128)(2,1)S(1)} %maximum_select_fusion.rest_0_), channel_id=1, source_target_pairs={{320,0},{288,32},{384,64},{352,96},{448,128},{416,160},{0,192},{48... | collective-permute-start | bytes 786440 | tf_op jit(solution)/shard_map/ppermute | solution.py:170
  53.9 10.0 %collective-permute-start.2 = (bf16[2,32,2,8,128]{4,3,2,1,0:T(8,128)(2,1)S(1)}, bf16[2,32,2,8,128]{4,3,2,1,0:T(8,128)(2,1)S(1)}, u32[]{:S(2)}, u32[]{:S(2)}) collective-permute-start(bf16[2,32,2,8,128]{4,3,2,1,0:T(8,128)(2,1)S(1)} %collective-permute-done.1.rest_0_), channel_id=1, source_target_pairs={{0,32},{32,0},{64,96},{96,64},{128,160},{160,128},{192,224},{224,1... | collective-permute-start | bytes 786440 | tf_op jit(solution)/shard_map/ppermute | solution.py:177
  58.2 5.7 %collective-permute-start.4 = (bf16[2,32,2,8,128]{4,3,2,1,0:T(8,128)(2,1)S(1)}, bf16[2,32,2,8,128]{4,3,2,1,0:T(8,128)(2,1)S(1)}, u32[]{:S(2)}, u32[]{:S(2)}) collective-permute-start(bf16[2,32,2,8,128]{4,3,2,1,0:T(8,128)(2,1)S(1)} %collective-permute-done.3.rest_1_), channel_id=1, source_target_pairs={{0,32},{32,0},{64,96},{96,64},{128,160},{160,128},{192,224},{224,1... | collective-permute-start | bytes 786440 | tf_op jit(solution)/shard_map/ppermute | solution.py:177
